TPU v7x, 512 devices: a whole 4x8x8 slice. The times are simulated.
512 devices in a mesh: gx: 32 (over y_hi, z, core), yz: 16 (over x, y_lo).
Axes of the slice: x: 4, y: 8 (y_hi: 2, y_lo: 4; y = y_hi * 4 + y_lo), z: 8, core: 2. Of those that a mesh axis runs over, the one named last changes fastest.
Arguments:
- gauge_links: float32 [64, 2, 3, 3, 2048], P('gx', None, None, None, 'yz'), may hold values from -1 to 1, as said below
- in_field: float32 [8, 64, 2, 3, 3, 2048], P(None, 'gx', None, None, None, 'yz'), may hold values from -6 to 6
- cotangent: float32 [8, 64, 2, 3, 3, 2048], P(None, 'gx', None, None, None, 'yz'), may hold values from -6 to 6
- bilinear_weights: float32 [8, 8, 24, 8], replicated, may hold values from -0.15625 to 0.15625
Outputs:
- grad_field: float32 [8, 64, 2, 3, 3, 2048], P(None, 'gx', None, None, None, 'yz')
- grad_weights: float32 [8, 8, 24, 8], replicated
Inputs may be any that keep to these rules, and one draw needn't show every extreme that they name: `gauge_links`: every site's link is a special unitary 3 x 3 matrix (unitary with determinant 1), stored as real and imaginary parts.
All inputs are finite; a program needn't handle non-finite values.
Results may differ from a plain program's by a relative error of at most 0.0003.
Values sent between devices are 32-bit elements; how exact they have to be, the bound alone decides.
No kernel may reach another device: no remote copies, remote signals or barrier semaphores. Data moves between devices by JAX's collectives and lax.ppermute only.
A program may use at most 64 MiB of HBM per device.

v0:
```python
import math
import jax
import jax.numpy as jnp
from jax import lax
from jax.sharding import PartitionSpec as P


def from_behind(block, axis, distance):
    devices = range(lax.axis_size(axis))
    route = [((i - distance) % len(devices), i) for i in devices]
    return lax.ppermute(block, axis, route)


def matmul_three(left, right):
    return jnp.sum(left[..., :, :, None, :] * right[..., None, :, :, :], axis=-3)


def complex_mul(left, right):
    left_re = left[..., 0, :, :, :]
    left_im = left[..., 1, :, :, :]
    right_re = right[..., 0, :, :, :]
    right_im = right[..., 1, :, :, :]
    real_part = matmul_three(left_re, right_re) - matmul_three(left_im, right_im)
    imag_part = matmul_three(left_re, right_im) + matmul_three(left_im, right_re)
    return jnp.stack([real_part, imag_part], axis=-4)


def dagger(matrix):
    swapped = jnp.swapaxes(matrix, -3, -2)
    return jnp.stack([swapped[..., 0, :, :, :], -swapped[..., 1, :, :, :]], axis=-4)


def per_device(gauge_links, in_field, cotangent, bilinear_weights):
    part_x = gauge_links.shape[0]
    channels = in_field.shape[0]
    line_count = bilinear_weights.shape[2]
    site_count = gauge_links.shape[-1]
    reach_devs = (part_x - 1 + line_count) // part_x
    highest = lax.Precision.HIGHEST
    weight_rows = bilinear_weights.reshape(channels * channels, line_count * channels)

    def advance(carry, unused):
        arrived = from_behind(carry, "gx", -1)
        return (arrived, arrived)

    unused_last, stacked = lax.scan(advance, (gauge_links, in_field), None, length=reach_devs)
    window_links = jnp.concatenate(
        [gauge_links, stacked[0].reshape((-1, 2, 3, 3, site_count))], axis=0
    )
    later_field = jnp.moveaxis(stacked[1], 0, 1).reshape((channels, -1, 2, 3, 3, site_count))
    window_field = jnp.concatenate([in_field, later_field], axis=1)
    pair_grad = complex_mul(dagger(in_field)[None], cotangent[:, None]).reshape(
        channels * channels, -1
    )

    def forward_step(line, offset):
        shifted = lax.dynamic_slice_in_dim(window_field, offset, part_x, axis=1)
        transported = complex_mul(complex_mul(line[None], shifted), dagger(line)[None])
        next_links = lax.dynamic_slice_in_dim(window_links, offset, part_x, axis=0)
        return (complex_mul(line, next_links), (transported, line))

    offsets = jnp.arange(1, line_count + 1, dtype=jnp.int32)
    unused_line, (all_transported, all_lines) = lax.scan(forward_step, gauge_links, offsets)
    transported_flat = all_transported.reshape(line_count * channels, -1)
    partial_grad = lax.dot_general(
        pair_grad, transported_flat, (((1,), (1,)), ((), ())), precision=highest
    )
    mixed = jnp.dot(weight_rows, transported_flat, precision=highest)
    mixed_matrix = mixed.reshape((channels, channels) + in_field.shape[1:])
    direct = jnp.sum(complex_mul(cotangent[:, None], dagger(mixed_matrix)), axis=0)
    line_grad = jnp.dot(weight_rows.T, pair_grad, precision=highest)
    line_grad = line_grad.reshape((line_count,) + in_field.shape)
    accumulator = jnp.zeros((channels, (reach_devs + 1) * part_x, 2, 3, 3, site_count), jnp.float32)

    def backward_step(carry, inputs):
        offset, grad_piece, line = inputs
        contribution = complex_mul(complex_mul(dagger(line)[None], grad_piece), line[None])
        current = lax.dynamic_slice_in_dim(carry, offset, part_x, axis=1)
        return (
            lax.dynamic_update_slice_in_dim(carry, current + contribution, offset, axis=1),
            None,
        )

    accumulator, unused_out = lax.scan(backward_step, accumulator, (offsets, line_grad, all_lines))
    blocks = jnp.moveaxis(
        accumulator.reshape((channels, reach_devs + 1, part_x, 2, 3, 3, site_count)), 1, 0
    )

    def return_step(carry, block):
        arrived = from_behind(carry, "gx", 1)
        return (arrived + block, None)

    far_terms, unused_tail = lax.scan(return_step, blocks[reach_devs], blocks[:reach_devs][::-1])
    grad_field = direct + far_terms
    total_x = part_x * lax.axis_size("gx")
    total_sites = site_count * lax.axis_size("yz")
    summed = lax.psum(partial_grad, ("gx", "yz"))
    grad_weights = summed.reshape(channels, channels, line_count, channels) / math.sqrt(
        100.0 * total_x * total_sites
    )
    return (grad_field, grad_weights)


def solution(mesh):
    placed = (
        P("gx", None, None, None, "yz"),
        P(None, "gx", None, None, None, "yz"),
        P(None, "gx", None, None, None, "yz"),
        P(),
    )
    return jax.shard_map(
        per_device,
        mesh=mesh,
        in_specs=placed,
        out_specs=(P(None, "gx", None, None, None, "yz"), P()),
        check_vma=False,
    )
```

profile of v0, /device:TPU:2, one launch (start us, length us, event | category | flops | bytes accessed | tf_op | source)
XLA Modules:
  0.0 771.0 jit_solution(7964423564091880756)
XLA Ops:
  2.4 183.7 %while.50 = (s32[]{:T(128)}, f32[2,2,3,3,128]{4,1,3,2,0:T(2,128)S(1)}, f32[8,2,2,3,3,128]{5,2,4,3,1,0:T(2,128)S(1)}, f32[12,2,2,3,3,128]{5,1,0,4,3,2:T(2,128)S(1...) while((s32[]{:T(128)}, f32[2,2,3,3,128]{4,1,3,2,0:T(2,128)S(1)}, ...), condition=%wide.region_1.2_spmd, body=%wide.region_0.1_spmd.sunk | while | flops 2 | bytes 1327269 | solution.py:46
  2.4 15.6 %collective-permute-start = (f32[2,2,3,3,128]{4,1,3,2,0:T(2,128)S(1)}, f32[2,2,3,3,128]{4,1,3,2,0:T(2,128)S(1)}, u32[]{:S(2)}, u32[]{:S(2)}) collective-permute-start(f32[2,2,3,3,128]{4,1,3,2,0:T(2,128)S(1)} %get-tuple-element.507), channel_id=1, source_target_pairs={{16,0},{32,16},{48,32},{64,48},{80,64},{96,80},{112,96},{128,112},... | collective-permute-start | bytes 55304 | tf_op jit(solution)/shard_map/while/body/eval_jaxpr/ppermute | solution.py:11
  18.0 2.6 collective-permute-start.1
  20.6 4.2 collective-permute-done.1
  24.9 9.8 %collective-permute-start = (f32[2,2,3,3,128]{4,1,3,2,0:T(2,128)S(1)}, f32[2,2,3,3,128]{4,1,3,2,0:T(2,128)S(1)}, u32[]{:S(2)}, u32[]{:S(2)}) collective-permute-start(f32[2,2,3,3,128]{4,1,3,2,0:T(2,128)S(1)} %get-tuple-element.507), channel_id=1, source_target_pairs={{16,0},{32,16},{48,32},{64,48},{80,64},{96,80},{112,96},{128,112},... | collective-permute-start | bytes 55304 | tf_op jit(solution)/shard_map/while/body/eval_jaxpr/ppermute | solution.py:11
  34.7 1.9 collective-permute-start.1
  36.7 3.9 collective-permute-done.1
  40.8 9.8 %collective-permute-start = (f32[2,2,3,3,128]{4,1,3,2,0:T(2,128)S(1)}, f32[2,2,3,3,128]{4,1,3,2,0:T(2,128)S(1)}, u32[]{:S(2)}, u32[]{:S(2)}) collective-permute-start(f32[2,2,3,3,128]{4,1,3,2,0:T(2,128)S(1)} %get-tuple-element.507), channel_id=1, source_target_pairs={{16,0},{32,16},{48,32},{64,48},{80,64},{96,80},{112,96},{128,112},... | collective-permute-start | bytes 55304 | tf_op jit(solution)/shard_map/while/body/eval_jaxpr/ppermute | solution.py:11
  50.6 1.9 collective-permute-start.1
  52.6 2.7 collective-permute-done.1
  55.4 9.8 %collective-permute-start = (f32[2,2,3,3,128]{4,1,3,2,0:T(2,128)S(1)}, f32[2,2,3,3,128]{4,1,3,2,0:T(2,128)S(1)}, u32[]{:S(2)}, u32[]{:S(2)}) collective-permute-start(f32[2,2,3,3,128]{4,1,3,2,0:T(2,128)S(1)} %get-tuple-element.507), channel_id=1, source_target_pairs={{16,0},{32,16},{48,32},{64,48},{80,64},{96,80},{112,96},{128,112},... | collective-permute-start | bytes 55304 | tf_op jit(solution)/shard_map/while/body/eval_jaxpr/ppermute | solution.py:11
  65.2 1.9 collective-permute-start.1
  67.2 2.6 collective-permute-done.1
  69.9 9.8 %collective-permute-start = (f32[2,2,3,3,128]{4,1,3,2,0:T(2,128)S(1)}, f32[2,2,3,3,128]{4,1,3,2,0:T(2,128)S(1)}, u32[]{:S(2)}, u32[]{:S(2)}) collective-permute-start(f32[2,2,3,3,128]{4,1,3,2,0:T(2,128)S(1)} %get-tuple-element.507), channel_id=1, source_target_pairs={{16,0},{32,16},{48,32},{64,48},{80,64},{96,80},{112,96},{128,112},... | collective-permute-start | bytes 55304 | tf_op jit(solution)/shard_map/while/body/eval_jaxpr/ppermute | solution.py:11
  79.8 1.9 collective-permute-start.1
  81.7 2.6 collective-permute-done.1
  84.4 9.8 %collective-permute-start = (f32[2,2,3,3,128]{4,1,3,2,0:T(2,128)S(1)}, f32[2,2,3,3,128]{4,1,3,2,0:T(2,128)S(1)}, u32[]{:S(2)}, u32[]{:S(2)}) collective-permute-start(f32[2,2,3,3,128]{4,1,3,2,0:T(2,128)S(1)} %get-tuple-element.507), channel_id=1, source_target_pairs={{16,0},{32,16},{48,32},{64,48},{80,64},{96,80},{112,96},{128,112},... | collective-permute-start | bytes 55304 | tf_op jit(solution)/shard_map/while/body/eval_jaxpr/ppermute | solution.py:11
  94.3 1.9 collective-permute-start.1
  96.3 2.6 collective-permute-done.1
  99.0 9.8 %collective-permute-start = (f32[2,2,3,3,128]{4,1,3,2,0:T(2,128)S(1)}, f32[2,2,3,3,128]{4,1,3,2,0:T(2,128)S(1)}, u32[]{:S(2)}, u32[]{:S(2)}) collective-permute-start(f32[2,2,3,3,128]{4,1,3,2,0:T(2,128)S(1)} %get-tuple-element.507), channel_id=1, source_target_pairs={{16,0},{32,16},{48,32},{64,48},{80,64},{96,80},{112,96},{128,112},... | collective-permute-start | bytes 55304 | tf_op jit(solution)/shard_map/while/body/eval_jaxpr/ppermute | solution.py:11
  108.8 1.9 collective-permute-start.1
  110.8 2.6 collective-permute-done.1
  113.5 9.8 %collective-permute-start = (f32[2,2,3,3,128]{4,1,3,2,0:T(2,128)S(1)}, f32[2,2,3,3,128]{4,1,3,2,0:T(2,128)S(1)}, u32[]{:S(2)}, u32[]{:S(2)}) collective-permute-start(f32[2,2,3,3,128]{4,1,3,2,0:T(2,128)S(1)} %get-tuple-element.507), channel_id=1, source_target_pairs={{16,0},{32,16},{48,32},{64,48},{80,64},{96,80},{112,96},{128,112},... | collective-permute-start | bytes 55304 | tf_op jit(solution)/shard_map/while/body/eval_jaxpr/ppermute | solution.py:11
  123.3 1.9 collective-permute-start.1
  125.3 2.6 collective-permute-done.1
  128.0 9.8 %collective-permute-start = (f32[2,2,3,3,128]{4,1,3,2,0:T(2,128)S(1)}, f32[2,2,3,3,128]{4,1,3,2,0:T(2,128)S(1)}, u32[]{:S(2)}, u32[]{:S(2)}) collective-permute-start(f32[2,2,3,3,128]{4,1,3,2,0:T(2,128)S(1)} %get-tuple-element.507), channel_id=1, source_target_pairs={{16,0},{32,16},{48,32},{64,48},{80,64},{96,80},{112,96},{128,112},... | collective-permute-start | bytes 55304 | tf_op jit(solution)/shard_map/while/body/eval_jaxpr/ppermute | solution.py:11
  137.8 1.9 collective-permute-start.1
  139.8 2.6 collective-permute-done.1
  142.5 9.8 %collective-permute-start = (f32[2,2,3,3,128]{4,1,3,2,0:T(2,128)S(1)}, f32[2,2,3,3,128]{4,1,3,2,0:T(2,128)S(1)}, u32[]{:S(2)}, u32[]{:S(2)}) collective-permute-start(f32[2,2,3,3,128]{4,1,3,2,0:T(2,128)S(1)} %get-tuple-element.507), channel_id=1, source_target_pairs={{16,0},{32,16},{48,32},{64,48},{80,64},{96,80},{112,96},{128,112},... | collective-permute-start | bytes 55304 | tf_op jit(solution)/shard_map/while/body/eval_jaxpr/ppermute | solution.py:11
  152.3 1.9 collective-permute-start.1
  154.3 2.6 collective-permute-done.1
  157.0 9.8 %collective-permute-start = (f32[2,2,3,3,128]{4,1,3,2,0:T(2,128)S(1)}, f32[2,2,3,3,128]{4,1,3,2,0:T(2,128)S(1)}, u32[]{:S(2)}, u32[]{:S(2)}) collective-permute-start(f32[2,2,3,3,128]{4,1,3,2,0:T(2,128)S(1)} %get-tuple-element.507), channel_id=1, source_target_pairs={{16,0},{32,16},{48,32},{64,48},{80,64},{96,80},{112,96},{128,112},... | collective-permute-start | bytes 55304 | tf_op jit(solution)/shard_map/while/body/eval_jaxpr/ppermute | solution.py:11
  166.9 1.9 collective-permute-start.1
  168.9 2.6 collective-permute-done.1
  171.6 9.8 %collective-permute-start = (f32[2,2,3,3,128]{4,1,3,2,0:T(2,128)S(1)}, f32[2,2,3,3,128]{4,1,3,2,0:T(2,128)S(1)}, u32[]{:S(2)}, u32[]{:S(2)}) collective-permute-start(f32[2,2,3,3,128]{4,1,3,2,0:T(2,128)S(1)} %get-tuple-element.507), channel_id=1, source_target_pairs={{16,0},{32,16},{48,32},{64,48},{80,64},{96,80},{112,96},{128,112},... | collective-permute-start | bytes 55304 | tf_op jit(solution)/shard_map/while/body/eval_jaxpr/ppermute | solution.py:11
  181.4 1.9 collective-permute-start.1
  183.4 2.6 collective-permute-done.1
  189.8 184.4 %while.51 = (s32[]{:T(128)}, f32[2,2,3,3,128]{4,0,3,2,1:T(2,128)}, f32[24,8,2,2,3,3,128]{6,1,5,4,3,2,0:T(8,128)S(1)}, f32[24,2,2,3,3,128]{5,1,4,3,2,0:T(2,128)},...) while((s32[]{:T(128)}, f32[2,2,3,3,128]{4,0,3,2,1:T(2,128)}, ...), condition=%wide.region_15.16_spmd, body=%wide.region_2.15_spmd.sunk | while | flops 910086 | bytes 2968279 | solution.py:63
  374.2 2.1 copy.70
  376.3 2.0 reshape.184
  378.3 3.3 fusion.5
  382.8 3.8 multiply_reduce_fusion.27
  387.9 4.2 fusion.7
  392.1 100.0 %psum.7 = f32[64,192]{1,0:T(8,128)S(1)} all-reduce(f32[64,192]{1,0:T(8,128)} %fusion.7), channel_id=1, replica_groups=mesh['gx'=32,'yz'=16] {'gx','yz'}, use_global_device_ids=true, to_apply=%region_37.38 | all-reduce | flops 12288 | bytes 98304 | tf_op jit(solution)/shard_map/psum | solution.py:97
  493.3 4.7 fusion.6
  498.1 104.9 %while.52 = (s32[]{:T(128)}, f32[8,26,2,3,3,128]{5,0,4,3,2,1:T(8,128)S(1)}, s32[24]{0:T(128)S(1)}, f32[24,2,2,3,3,128]{5,1,4,3,2,0:T(2,128)}, f32[24,8,2,2,3,3,1...) while((s32[]{:T(128)}, f32[8,26,2,3,3,128]{5,0,4,3,2,1:T(8,128)S(1)}, s32[24]{0:T(128)S(1)}, ...), condition=%wide.region_34.35_spmd, body=%wide.region_25.34_spmd.sunk | while | flops 891653 | bytes 3411083 | solution.py:84
  604.4 2.9 rev.3
  607.3 161.5 %while.53 = (s32[]{:T(128)}, f32[8,2,2,3,3,128]{5,4,3,2,1,0:T(4,128)S(1)}, f32[12,8,2,2,3,3,128]{6,1,5,4,3,2,0:T(8,128)}, s32[]{:T(128)}) while((s32[]{:T(128)}, f32[8,2,2,3,3,128]{5,4,3,2,1,0:T(4,128)S(1)}, f32[12,8,2,2,3,3,128]{6,1,5,4,3,2,0:T(8,128)}, s32[]{:T(128)}) %tuple.163), condition=%wide.region_36.37_spmd, body=%wide.region_35.36_spmd.sunk | while | flops 36866 | bytes 1327209 | solution.py:93
  607.3 2.1 collective-permute-start.2
  610.3 12.3 %collective-permute-done.2 = f32[8,2,2,3,3,128]{5,4,3,2,1,0:T(4,128)S(1)} collective-permute-done((f32[8,2,2,3,3,128]{5,4,3,2,1,0:T(4,128)S(1)}, f32[8,2,2,3,3,128]{5,4,3,2,1,0:T(4,128)S(1)}, u32[]{:S(2)}, u32[]{:S(2)}) %collective-permute-start.2) | collective-permute-done | bytes 147488 | tf_op jit(solution)/shard_map/while/body/eval_jaxpr/ppermute | solution.py:11
  625.5 12.2 %collective-permute-done.2 = f32[8,2,2,3,3,128]{5,4,3,2,1,0:T(4,128)S(1)} collective-permute-done((f32[8,2,2,3,3,128]{5,4,3,2,1,0:T(4,128)S(1)}, f32[8,2,2,3,3,128]{5,4,3,2,1,0:T(4,128)S(1)}, u32[]{:S(2)}, u32[]{:S(2)}) %collective-permute-start.2) | collective-permute-done | bytes 147488 | tf_op jit(solution)/shard_map/while/body/eval_jaxpr/ppermute | solution.py:11
  640.7 10.2 %collective-permute-done.2 = f32[8,2,2,3,3,128]{5,4,3,2,1,0:T(4,128)S(1)} collective-permute-done((f32[8,2,2,3,3,128]{5,4,3,2,1,0:T(4,128)S(1)}, f32[8,2,2,3,3,128]{5,4,3,2,1,0:T(4,128)S(1)}, u32[]{:S(2)}, u32[]{:S(2)}) %collective-permute-start.2) | collective-permute-done | bytes 147488 | tf_op jit(solution)/shard_map/while/body/eval_jaxpr/ppermute | solution.py:11
  651.1 1.9 collective-permute-start.2
  653.9 10.2 %collective-permute-done.2 = f32[8,2,2,3,3,128]{5,4,3,2,1,0:T(4,128)S(1)} collective-permute-done((f32[8,2,2,3,3,128]{5,4,3,2,1,0:T(4,128)S(1)}, f32[8,2,2,3,3,128]{5,4,3,2,1,0:T(4,128)S(1)}, u32[]{:S(2)}, u32[]{:S(2)}) %collective-permute-start.2) | collective-permute-done | bytes 147488 | tf_op jit(solution)/shard_map/while/body/eval_jaxpr/ppermute | solution.py:11
  667.0 10.1 %collective-permute-done.2 = f32[8,2,2,3,3,128]{5,4,3,2,1,0:T(4,128)S(1)} collective-permute-done((f32[8,2,2,3,3,128]{5,4,3,2,1,0:T(4,128)S(1)}, f32[8,2,2,3,3,128]{5,4,3,2,1,0:T(4,128)S(1)}, u32[]{:S(2)}, u32[]{:S(2)}) %collective-permute-start.2) | collective-permute-done | bytes 147488 | tf_op jit(solution)/shard_map/while/body/eval_jaxpr/ppermute | solution.py:11
  677.2 1.9 collective-permute-start.2
  680.1 10.1 %collective-permute-done.2 = f32[8,2,2,3,3,128]{5,4,3,2,1,0:T(4,128)S(1)} collective-permute-done((f32[8,2,2,3,3,128]{5,4,3,2,1,0:T(4,128)S(1)}, f32[8,2,2,3,3,128]{5,4,3,2,1,0:T(4,128)S(1)}, u32[]{:S(2)}, u32[]{:S(2)}) %collective-permute-start.2) | collective-permute-done | bytes 147488 | tf_op jit(solution)/shard_map/while/body/eval_jaxpr/ppermute | solution.py:11
  693.2 10.1 %collective-permute-done.2 = f32[8,2,2,3,3,128]{5,4,3,2,1,0:T(4,128)S(1)} collective-permute-done((f32[8,2,2,3,3,128]{5,4,3,2,1,0:T(4,128)S(1)}, f32[8,2,2,3,3,128]{5,4,3,2,1,0:T(4,128)S(1)}, u32[]{:S(2)}, u32[]{:S(2)}) %collective-permute-start.2) | collective-permute-done | bytes 147488 | tf_op jit(solution)/shard_map/while/body/eval_jaxpr/ppermute | solution.py:11
  706.3 10.1 %collective-permute-done.2 = f32[8,2,2,3,3,128]{5,4,3,2,1,0:T(4,128)S(1)} collective-permute-done((f32[8,2,2,3,3,128]{5,4,3,2,1,0:T(4,128)S(1)}, f32[8,2,2,3,3,128]{5,4,3,2,1,0:T(4,128)S(1)}, u32[]{:S(2)}, u32[]{:S(2)}) %collective-permute-start.2) | collective-permute-done | bytes 147488 | tf_op jit(solution)/shard_map/while/body/eval_jaxpr/ppermute | solution.py:11
  719.4 10.1 %collective-permute-done.2 = f32[8,2,2,3,3,128]{5,4,3,2,1,0:T(4,128)S(1)} collective-permute-done((f32[8,2,2,3,3,128]{5,4,3,2,1,0:T(4,128)S(1)}, f32[8,2,2,3,3,128]{5,4,3,2,1,0:T(4,128)S(1)}, u32[]{:S(2)}, u32[]{:S(2)}) %collective-permute-start.2) | collective-permute-done | bytes 147488 | tf_op jit(solution)/shard_map/while/body/eval_jaxpr/ppermute | solution.py:11
  729.6 1.9 collective-permute-start.2
  732.5 10.1 %collective-permute-done.2 = f32[8,2,2,3,3,128]{5,4,3,2,1,0:T(4,128)S(1)} collective-permute-done((f32[8,2,2,3,3,128]{5,4,3,2,1,0:T(4,128)S(1)}, f32[8,2,2,3,3,128]{5,4,3,2,1,0:T(4,128)S(1)}, u32[]{:S(2)}, u32[]{:S(2)}) %collective-permute-start.2) | collective-permute-done | bytes 147488 | tf_op jit(solution)/shard_map/while/body/eval_jaxpr/ppermute | solution.py:11
  745.6 10.1 %collective-permute-done.2 = f32[8,2,2,3,3,128]{5,4,3,2,1,0:T(4,128)S(1)} collective-permute-done((f32[8,2,2,3,3,128]{5,4,3,2,1,0:T(4,128)S(1)}, f32[8,2,2,3,3,128]{5,4,3,2,1,0:T(4,128)S(1)}, u32[]{:S(2)}, u32[]{:S(2)}) %collective-permute-start.2) | collective-permute-done | bytes 147488 | tf_op jit(solution)/shard_map/while/body/eval_jaxpr/ppermute | solution.py:11
  758.7 10.1 %collective-permute-done.2 = f32[8,2,2,3,3,128]{5,4,3,2,1,0:T(4,128)S(1)} collective-permute-done((f32[8,2,2,3,3,128]{5,4,3,2,1,0:T(4,128)S(1)}, f32[8,2,2,3,3,128]{5,4,3,2,1,0:T(4,128)S(1)}, u32[]{:S(2)}, u32[]{:S(2)}) %collective-permute-start.2) | collective-permute-done | bytes 147488 | tf_op jit(solution)/shard_map/while/body/eval_jaxpr/ppermute | solution.py:11
  (1181 shorter events, 234.8 us)
Async XLA Ops:
  1.6 184.5 %copy-start.11 = (f32[2,2,3,3,128]{4,1,3,2,0:T(2,128)S(1)}, f32[2,2,3,3,128]{4,1,3,2,0:T(2,128)}, u32[]{:S(2)}) copy-start(f32[2,2,3,3,128]{4,1,3,2,0:T(2,128)} %param.12) | copy-start | bytes 55300
  2.4 18.2 %collective-permute-start = (f32[2,2,3,3,128]{4,1,3,2,0:T(2,128)S(1)}, f32[2,2,3,3,128]{4,1,3,2,0:T(2,128)S(1)}, u32[]{:S(2)}, u32[]{:S(2)}) collective-permute-start(f32[2,2,3,3,128]{4,1,3,2,0:T(2,128)S(1)} %get-tuple-element.507), channel_id=1, source_target_pairs={{16,0},{32,16},{48,32},{64,48},{80,64},{96,80},{112,96},{128,112},... | collective-permute-start | bytes 55304 | tf_op jit(solution)/shard_map/while/body/eval_jaxpr/ppermute | solution.py:11
  18.0 6.8 collective-permute-start.1
  24.9 11.7 %collective-permute-start = (f32[2,2,3,3,128]{4,1,3,2,0:T(2,128)S(1)}, f32[2,2,3,3,128]{4,1,3,2,0:T(2,128)S(1)}, u32[]{:S(2)}, u32[]{:S(2)}) collective-permute-start(f32[2,2,3,3,128]{4,1,3,2,0:T(2,128)S(1)} %get-tuple-element.507), channel_id=1, source_target_pairs={{16,0},{32,16},{48,32},{64,48},{80,64},{96,80},{112,96},{128,112},... | collective-permute-start | bytes 55304 | tf_op jit(solution)/shard_map/while/body/eval_jaxpr/ppermute | solution.py:11
  34.7 5.9 collective-permute-start.1
  40.8 11.8 %collective-permute-start = (f32[2,2,3,3,128]{4,1,3,2,0:T(2,128)S(1)}, f32[2,2,3,3,128]{4,1,3,2,0:T(2,128)S(1)}, u32[]{:S(2)}, u32[]{:S(2)}) collective-permute-start(f32[2,2,3,3,128]{4,1,3,2,0:T(2,128)S(1)} %get-tuple-element.507), channel_id=1, source_target_pairs={{16,0},{32,16},{48,32},{64,48},{80,64},{96,80},{112,96},{128,112},... | collective-permute-start | bytes 55304 | tf_op jit(solution)/shard_map/while/body/eval_jaxpr/ppermute | solution.py:11
  50.6 4.7 collective-permute-start.1
  55.4 11.8 %collective-permute-start = (f32[2,2,3,3,128]{4,1,3,2,0:T(2,128)S(1)}, f32[2,2,3,3,128]{4,1,3,2,0:T(2,128)S(1)}, u32[]{:S(2)}, u32[]{:S(2)}) collective-permute-start(f32[2,2,3,3,128]{4,1,3,2,0:T(2,128)S(1)} %get-tuple-element.507), channel_id=1, source_target_pairs={{16,0},{32,16},{48,32},{64,48},{80,64},{96,80},{112,96},{128,112},... | collective-permute-start | bytes 55304 | tf_op jit(solution)/shard_map/while/body/eval_jaxpr/ppermute | solution.py:11
  65.2 4.6 collective-permute-start.1
  69.9 11.8 %collective-permute-start = (f32[2,2,3,3,128]{4,1,3,2,0:T(2,128)S(1)}, f32[2,2,3,3,128]{4,1,3,2,0:T(2,128)S(1)}, u32[]{:S(2)}, u32[]{:S(2)}) collective-permute-start(f32[2,2,3,3,128]{4,1,3,2,0:T(2,128)S(1)} %get-tuple-element.507), channel_id=1, source_target_pairs={{16,0},{32,16},{48,32},{64,48},{80,64},{96,80},{112,96},{128,112},... | collective-permute-start | bytes 55304 | tf_op jit(solution)/shard_map/while/body/eval_jaxpr/ppermute | solution.py:11
  79.8 4.6 collective-permute-start.1
  84.4 11.8 %collective-permute-start = (f32[2,2,3,3,128]{4,1,3,2,0:T(2,128)S(1)}, f32[2,2,3,3,128]{4,1,3,2,0:T(2,128)S(1)}, u32[]{:S(2)}, u32[]{:S(2)}) collective-permute-start(f32[2,2,3,3,128]{4,1,3,2,0:T(2,128)S(1)} %get-tuple-element.507), channel_id=1, source_target_pairs={{16,0},{32,16},{48,32},{64,48},{80,64},{96,80},{112,96},{128,112},... | collective-permute-start | bytes 55304 | tf_op jit(solution)/shard_map/while/body/eval_jaxpr/ppermute | solution.py:11
  94.3 4.6 collective-permute-start.1
  99.0 11.8 %collective-permute-start = (f32[2,2,3,3,128]{4,1,3,2,0:T(2,128)S(1)}, f32[2,2,3,3,128]{4,1,3,2,0:T(2,128)S(1)}, u32[]{:S(2)}, u32[]{:S(2)}) collective-permute-start(f32[2,2,3,3,128]{4,1,3,2,0:T(2,128)S(1)} %get-tuple-element.507), channel_id=1, source_target_pairs={{16,0},{32,16},{48,32},{64,48},{80,64},{96,80},{112,96},{128,112},... | collective-permute-start | bytes 55304 | tf_op jit(solution)/shard_map/while/body/eval_jaxpr/ppermute | solution.py:11
  108.8 4.6 collective-permute-start.1
  113.5 11.8 %collective-permute-start = (f32[2,2,3,3,128]{4,1,3,2,0:T(2,128)S(1)}, f32[2,2,3,3,128]{4,1,3,2,0:T(2,128)S(1)}, u32[]{:S(2)}, u32[]{:S(2)}) collective-permute-start(f32[2,2,3,3,128]{4,1,3,2,0:T(2,128)S(1)} %get-tuple-element.507), channel_id=1, source_target_pairs={{16,0},{32,16},{48,32},{64,48},{80,64},{96,80},{112,96},{128,112},... | collective-permute-start | bytes 55304 | tf_op jit(solution)/shard_map/while/body/eval_jaxpr/ppermute | solution.py:11
  123.3 4.6 collective-permute-start.1
  128.0 11.8 %collective-permute-start = (f32[2,2,3,3,128]{4,1,3,2,0:T(2,128)S(1)}, f32[2,2,3,3,128]{4,1,3,2,0:T(2,128)S(1)}, u32[]{:S(2)}, u32[]{:S(2)}) collective-permute-start(f32[2,2,3,3,128]{4,1,3,2,0:T(2,128)S(1)} %get-tuple-element.507), channel_id=1, source_target_pairs={{16,0},{32,16},{48,32},{64,48},{80,64},{96,80},{112,96},{128,112},... | collective-permute-start | bytes 55304 | tf_op jit(solution)/shard_map/while/body/eval_jaxpr/ppermute | solution.py:11
  137.8 4.6 collective-permute-start.1
  142.5 11.8 %collective-permute-start = (f32[2,2,3,3,128]{4,1,3,2,0:T(2,128)S(1)}, f32[2,2,3,3,128]{4,1,3,2,0:T(2,128)S(1)}, u32[]{:S(2)}, u32[]{:S(2)}) collective-permute-start(f32[2,2,3,3,128]{4,1,3,2,0:T(2,128)S(1)} %get-tuple-element.507), channel_id=1, source_target_pairs={{16,0},{32,16},{48,32},{64,48},{80,64},{96,80},{112,96},{128,112},... | collective-permute-start | bytes 55304 | tf_op jit(solution)/shard_map/while/body/eval_jaxpr/ppermute | solution.py:11
  152.3 4.6 collective-permute-start.1
  157.0 11.8 %collective-permute-start = (f32[2,2,3,3,128]{4,1,3,2,0:T(2,128)S(1)}, f32[2,2,3,3,128]{4,1,3,2,0:T(2,128)S(1)}, u32[]{:S(2)}, u32[]{:S(2)}) collective-permute-start(f32[2,2,3,3,128]{4,1,3,2,0:T(2,128)S(1)} %get-tuple-element.507), channel_id=1, source_target_pairs={{16,0},{32,16},{48,32},{64,48},{80,64},{96,80},{112,96},{128,112},... | collective-permute-start | bytes 55304 | tf_op jit(solution)/shard_map/while/body/eval_jaxpr/ppermute | solution.py:11
  166.9 4.6 collective-permute-start.1
  171.6 11.8 %collective-permute-start = (f32[2,2,3,3,128]{4,1,3,2,0:T(2,128)S(1)}, f32[2,2,3,3,128]{4,1,3,2,0:T(2,128)S(1)}, u32[]{:S(2)}, u32[]{:S(2)}) collective-permute-start(f32[2,2,3,3,128]{4,1,3,2,0:T(2,128)S(1)} %get-tuple-element.507), channel_id=1, source_target_pairs={{16,0},{32,16},{48,32},{64,48},{80,64},{96,80},{112,96},{128,112},... | collective-permute-start | bytes 55304 | tf_op jit(solution)/shard_map/while/body/eval_jaxpr/ppermute | solution.py:11
  181.4 4.6 collective-permute-start.1
  192.5 2.7 copy-start.3
  200.2 2.7 copy-start.3
  207.9 2.7 copy-start.3
  215.6 2.7 copy-start.3
  223.2 2.7 copy-start.3
  230.9 2.7 copy-start.3
  238.6 2.7 copy-start.3
  246.3 2.7 copy-start.3
  254.0 2.7 copy-start.3
  261.7 2.7 copy-start.3
  269.4 2.7 copy-start.3
  277.1 2.7 copy-start.3
  284.8 2.7 copy-start.3
  292.4 2.7 copy-start.3
  300.1 2.7 copy-start.3
  307.8 2.7 copy-start.3
  315.5 2.7 copy-start.3
  323.2 2.7 copy-start.3
  330.9 2.7 copy-start.3
  338.6 2.7 copy-start.3
  346.3 2.7 copy-start.3
  353.9 2.7 copy-start.3
  392.1 101.2 %copy-start.1 = (f32[8,8,2,2,3,3,128]{6,1,5,4,3,2,0:T(8,128)S(1)}, f32[8,8,2,2,3,3,128]{6,1,5,4,3,2,0:T(8,128)}, u32[]{:S(2)}) copy-start(f32[8,8,2,2,3,3,128]{6,1,5,4,3,2,0:T(8,128)} %copy-done) | copy-start | bytes 3538948
  392.1 101.2 %copy-start.9 = (f32[64,192]{1,0:T(8,128)S(1)}, f32[64,192]{1,0:T(8,128)}, u32[]{:S(2)}) copy-start(f32[64,192]{1,0:T(8,128)} %reshape.184) | copy-start | bytes 147460
  604.4 164.5 %copy-start.6 = (f32[8,8,2,3,3,128]{5,1,4,3,2,0:T(8,128)S(1)}, f32[8,8,2,3,3,128]{5,1,4,3,2,0:T(8,128)}, u32[]{:S(2)}) copy-start(f32[8,8,2,3,3,128]{5,1,4,3,2,0:T(8,128)} %get-tuple-element.198) | copy-start | bytes 1769476
  607.2 161.6 %copy-start.5 = (f32[8,8,2,3,3,128]{5,1,4,3,2,0:T(8,128)S(1)}, f32[8,8,2,3,3,128]{5,1,4,3,2,0:T(8,128)}, u32[]{:S(2)}) copy-start(f32[8,8,2,3,3,128]{5,1,4,3,2,0:T(8,128)} %get-tuple-element.197) | copy-start | bytes 1769476
  607.3 161.6 %copy-start.4 = (f32[8,8,2,3,3,128]{5,1,4,3,2,0:T(8,128)S(1)}, f32[8,8,2,3,3,128]{5,1,4,3,2,0:T(8,128)}, u32[]{:S(2)}) copy-start(f32[8,8,2,3,3,128]{5,1,4,3,2,0:T(8,128)} %get-tuple-element.196) | copy-start | bytes 1769476
  607.3 15.2 %collective-permute-start.2 = (f32[8,2,2,3,3,128]{5,4,3,2,1,0:T(4,128)S(1)}, f32[8,2,2,3,3,128]{5,4,3,2,1,0:T(4,128)S(1)}, u32[]{:S(2)}, u32[]{:S(2)}) collective-permute-start(f32[8,2,2,3,3,128]{5,4,3,2,1,0:T(4,128)S(1)} %get-tuple-element.580), channel_id=1, source_target_pairs={{496,0},{0,16},{16,32},{32,48},{48,64},{64,80},{80,96},{96,112},{1... | collective-permute-start | bytes 442376 | tf_op jit(solution)/shard_map/while/body/eval_jaxpr/ppermute | solution.py:11
  622.7 15.1 %collective-permute-start.2 = (f32[8,2,2,3,3,128]{5,4,3,2,1,0:T(4,128)S(1)}, f32[8,2,2,3,3,128]{5,4,3,2,1,0:T(4,128)S(1)}, u32[]{:S(2)}, u32[]{:S(2)}) collective-permute-start(f32[8,2,2,3,3,128]{5,4,3,2,1,0:T(4,128)S(1)} %get-tuple-element.580), channel_id=1, source_target_pairs={{496,0},{0,16},{16,32},{32,48},{48,64},{64,80},{80,96},{96,112},{1... | collective-permute-start | bytes 442376 | tf_op jit(solution)/shard_map/while/body/eval_jaxpr/ppermute | solution.py:11
  637.9 13.1 %collective-permute-start.2 = (f32[8,2,2,3,3,128]{5,4,3,2,1,0:T(4,128)S(1)}, f32[8,2,2,3,3,128]{5,4,3,2,1,0:T(4,128)S(1)}, u32[]{:S(2)}, u32[]{:S(2)}) collective-permute-start(f32[8,2,2,3,3,128]{5,4,3,2,1,0:T(4,128)S(1)} %get-tuple-element.580), channel_id=1, source_target_pairs={{496,0},{0,16},{16,32},{32,48},{48,64},{64,80},{80,96},{96,112},{1... | collective-permute-start | bytes 442376 | tf_op jit(solution)/shard_map/while/body/eval_jaxpr/ppermute | solution.py:11
  651.1 13.0 %collective-permute-start.2 = (f32[8,2,2,3,3,128]{5,4,3,2,1,0:T(4,128)S(1)}, f32[8,2,2,3,3,128]{5,4,3,2,1,0:T(4,128)S(1)}, u32[]{:S(2)}, u32[]{:S(2)}) collective-permute-start(f32[8,2,2,3,3,128]{5,4,3,2,1,0:T(4,128)S(1)} %get-tuple-element.580), channel_id=1, source_target_pairs={{496,0},{0,16},{16,32},{32,48},{48,64},{64,80},{80,96},{96,112},{1... | collective-permute-start | bytes 442376 | tf_op jit(solution)/shard_map/while/body/eval_jaxpr/ppermute | solution.py:11
  664.2 13.0 %collective-permute-start.2 = (f32[8,2,2,3,3,128]{5,4,3,2,1,0:T(4,128)S(1)}, f32[8,2,2,3,3,128]{5,4,3,2,1,0:T(4,128)S(1)}, u32[]{:S(2)}, u32[]{:S(2)}) collective-permute-start(f32[8,2,2,3,3,128]{5,4,3,2,1,0:T(4,128)S(1)} %get-tuple-element.580), channel_id=1, source_target_pairs={{496,0},{0,16},{16,32},{32,48},{48,64},{64,80},{80,96},{96,112},{1... | collective-permute-start | bytes 442376 | tf_op jit(solution)/shard_map/while/body/eval_jaxpr/ppermute | solution.py:11
  677.2 13.0 %collective-permute-start.2 = (f32[8,2,2,3,3,128]{5,4,3,2,1,0:T(4,128)S(1)}, f32[8,2,2,3,3,128]{5,4,3,2,1,0:T(4,128)S(1)}, u32[]{:S(2)}, u32[]{:S(2)}) collective-permute-start(f32[8,2,2,3,3,128]{5,4,3,2,1,0:T(4,128)S(1)} %get-tuple-element.580), channel_id=1, source_target_pairs={{496,0},{0,16},{16,32},{32,48},{48,64},{64,80},{80,96},{96,112},{1... | collective-permute-start | bytes 442376 | tf_op jit(solution)/shard_map/while/body/eval_jaxpr/ppermute | solution.py:11
  690.3 13.0 %collective-permute-start.2 = (f32[8,2,2,3,3,128]{5,4,3,2,1,0:T(4,128)S(1)}, f32[8,2,2,3,3,128]{5,4,3,2,1,0:T(4,128)S(1)}, u32[]{:S(2)}, u32[]{:S(2)}) collective-permute-start(f32[8,2,2,3,3,128]{5,4,3,2,1,0:T(4,128)S(1)} %get-tuple-element.580), channel_id=1, source_target_pairs={{496,0},{0,16},{16,32},{32,48},{48,64},{64,80},{80,96},{96,112},{1... | collective-permute-start | bytes 442376 | tf_op jit(solution)/shard_map/while/body/eval_jaxpr/ppermute | solution.py:11
  703.4 13.0 %collective-permute-start.2 = (f32[8,2,2,3,3,128]{5,4,3,2,1,0:T(4,128)S(1)}, f32[8,2,2,3,3,128]{5,4,3,2,1,0:T(4,128)S(1)}, u32[]{:S(2)}, u32[]{:S(2)}) collective-permute-start(f32[8,2,2,3,3,128]{5,4,3,2,1,0:T(4,128)S(1)} %get-tuple-element.580), channel_id=1, source_target_pairs={{496,0},{0,16},{16,32},{32,48},{48,64},{64,80},{80,96},{96,112},{1... | collective-permute-start | bytes 442376 | tf_op jit(solution)/shard_map/while/body/eval_jaxpr/ppermute | solution.py:11
  716.5 13.0 %collective-permute-start.2 = (f32[8,2,2,3,3,128]{5,4,3,2,1,0:T(4,128)S(1)}, f32[8,2,2,3,3,128]{5,4,3,2,1,0:T(4,128)S(1)}, u32[]{:S(2)}, u32[]{:S(2)}) collective-permute-start(f32[8,2,2,3,3,128]{5,4,3,2,1,0:T(4,128)S(1)} %get-tuple-element.580), channel_id=1, source_target_pairs={{496,0},{0,16},{16,32},{32,48},{48,64},{64,80},{80,96},{96,112},{1... | collective-permute-start | bytes 442376 | tf_op jit(solution)/shard_map/while/body/eval_jaxpr/ppermute | solution.py:11
  729.6 13.0 %collective-permute-start.2 = (f32[8,2,2,3,3,128]{5,4,3,2,1,0:T(4,128)S(1)}, f32[8,2,2,3,3,128]{5,4,3,2,1,0:T(4,128)S(1)}, u32[]{:S(2)}, u32[]{:S(2)}) collective-permute-start(f32[8,2,2,3,3,128]{5,4,3,2,1,0:T(4,128)S(1)} %get-tuple-element.580), channel_id=1, source_target_pairs={{496,0},{0,16},{16,32},{32,48},{48,64},{64,80},{80,96},{96,112},{1... | collective-permute-start | bytes 442376 | tf_op jit(solution)/shard_map/while/body/eval_jaxpr/ppermute | solution.py:11
  742.7 13.0 %collective-permute-start.2 = (f32[8,2,2,3,3,128]{5,4,3,2,1,0:T(4,128)S(1)}, f32[8,2,2,3,3,128]{5,4,3,2,1,0:T(4,128)S(1)}, u32[]{:S(2)}, u32[]{:S(2)}) collective-permute-start(f32[8,2,2,3,3,128]{5,4,3,2,1,0:T(4,128)S(1)} %get-tuple-element.580), channel_id=1, source_target_pairs={{496,0},{0,16},{16,32},{32,48},{48,64},{64,80},{80,96},{96,112},{1... | collective-permute-start | bytes 442376 | tf_op jit(solution)/shard_map/while/body/eval_jaxpr/ppermute | solution.py:11
  755.8 13.0 %collective-permute-start.2 = (f32[8,2,2,3,3,128]{5,4,3,2,1,0:T(4,128)S(1)}, f32[8,2,2,3,3,128]{5,4,3,2,1,0:T(4,128)S(1)}, u32[]{:S(2)}, u32[]{:S(2)}) collective-permute-start(f32[8,2,2,3,3,128]{5,4,3,2,1,0:T(4,128)S(1)} %get-tuple-element.580), channel_id=1, source_target_pairs={{496,0},{0,16},{16,32},{32,48},{48,64},{64,80},{80,96},{96,112},{1... | collective-permute-start | bytes 442376 | tf_op jit(solution)/shard_map/while/body/eval_jaxpr/ppermute | solution.py:11
  (7 other events, 9.9 us)
where the time goes:
time: 780 us; the launch traced here: 771 us
  local copies, waits for them, and re-layouts  177 us (23%)
  starting transfers between devices  171 us (22%)
  waiting for transfers between devices  160 us (21%)
  blocking collectives  100 us (13%)
  loops' own time  96.8 us (12%)
  other arithmetic  53.1 us (7%)
  matrix products  12.2 us (2%)
    ppermute x36, starting transfers between devices, from_behind(): return lax.ppermute(block, axis, route)  171 us
    ppermute x36, waiting for transfers between devices, from_behind(): return lax.ppermute(block, axis, route)  160 us
    psum x1, blocking collectives, per_device(): summed = lax.psum(partial_grad, ('gx', 'yz'))  100 us
    mul x364, local copies, waits for them, and re-layouts, matmul_three(): left[..., :, :, None, :] * right[..., None, :, :, :]  64.4 us
    another operation x1, loops' own time, per_device(): lax.scan(forward_step, gauge_links, offsets)  51.7 us
    another operation x1, loops' own time, per_device(): lax.scan(backward_step, accumulator, (offsets, line_grad, all_lines))  44 us
    dynamic_slice x48, local copies, waits for them, and re-layouts, per_device(): lax.scan(forward_step, gauge_links, offsets)  29.5 us
    squeeze x24, local copies, waits for them, and re-layouts, per_device(): lax.scan(backward_step, accumulator, (offsets, line_grad, all_lines))  22.2 us
  transfers between devices with their start and end apart: 36, of which 24 were waited for; matrix products, arithmetic and copies ran while one was open for 1% of the time, Pallas kernels for 0%

commit v1 on v0

--- a/solution.py
+++ b/solution.py
@@ -3,6 +3,12 @@
 import jax.numpy as jnp
 from jax import lax
 from jax.sharding import PartitionSpec as P
+
+
+def summed_here(value, axis):
+    parts = lax.all_gather(value, axis, axis=0, tiled=False)
+    acc = parts.sum(axis=0)
+    return acc
 
 
 def from_behind(block, axis, distance):
@@ -94,7 +100,7 @@
     grad_field = direct + far_terms
     total_x = part_x * lax.axis_size("gx")
     total_sites = site_count * lax.axis_size("yz")
-    summed = lax.psum(partial_grad, ("gx", "yz"))
+    summed = summed_here(partial_grad, ("gx", "yz"))
     grad_weights = summed.reshape(channels, channels, line_count, channels) / math.sqrt(
         100.0 * total_x * total_sites
     )

time: 780 us -> 1980 us (2.54)
  the two profiles are of different devices: /device:TPU:2 before, /device:TPU:473 now
where the time goes in v1:
time: 1980 us; the launch traced here: 1970 us
  waiting for transfers between devices  1360 us (69%)
  local copies, waits for them, and re-layouts  216 us (11%)
  starting transfers between devices  164 us (8%)
  loops' own time  99 us (5%)
  other arithmetic  97.2 us (5%)
    all_gather x1, waiting for transfers between devices, summed_here(): parts = lax.all_gather(value, axis, axis=0, tiled=False)  1200 us
    ppermute x36, starting transfers between devices, from_behind(): return lax.ppermute(block, axis, route)  164 us
    ppermute x36, waiting for transfers between devices, from_behind(): return lax.ppermute(block, axis, route)  160 us
    mul x364, local copies, waits for them, and re-layouts, matmul_three(): left[..., :, :, None, :] * right[..., None, :, :, :]  97.3 us
    another operation x1, loops' own time, per_device(): lax.scan(backward_step, accumulator, (offsets, line_grad, all_lines))  49.8 us
    another operation x1, loops' own time, per_device(): lax.scan(forward_step, gauge_links, offsets)  48.2 us
  transfers between devices with their start and end apart: 37, of which 37 were waited for; matrix products, arithmetic and copies ran while one was open for 4% of the time, Pallas kernels for 0%

profile of v1, /device:TPU:473, one launch (start us, length us, event | category | flops | bytes accessed | tf_op | source)
XLA Modules:
  0.0 1967.3 jit_solution(2745664473801611769)
XLA Ops:
  12.6 177.0 %while.50 = (s32[]{:T(128)}, f32[2,2,3,3,128]{4,1,3,2,0:T(2,128)S(1)}, f32[8,2,2,3,3,128]{5,2,4,3,1,0:T(2,128)S(1)}, f32[12,2,2,3,3,128]{5,1,0,4,3,2:T(2,128)S(1...) while((s32[]{:T(128)}, f32[2,2,3,3,128]{4,1,3,2,0:T(2,128)S(1)}, ...), condition=%wide.region_1.2_spmd, body=%wide.region_0.1_spmd.sunk | while | flops 2 | bytes 1327269 | solution.py:52
  12.6 2.6 collective-permute-start
  15.2 1.9 collective-permute-start.1
  17.1 6.6 collective-permute-done
  23.7 3.9 collective-permute-done.1
  31.6 7.3 collective-permute-done
  38.9 3.5 collective-permute-done.1
  42.5 1.9 collective-permute-start
  44.4 1.9 collective-permute-start.1
  46.3 7.3 collective-permute-done
  53.6 3.5 collective-permute-done.1
  61.0 7.3 collective-permute-done
  68.3 3.5 collective-permute-done.1
  73.8 1.9 collective-permute-start.1
  75.8 7.3 collective-permute-done
  83.0 3.5 collective-permute-done.1
  90.5 7.3 collective-permute-done
  97.8 3.5 collective-permute-done.1
  105.2 7.3 collective-permute-done
  112.5 3.5 collective-permute-done.1
  119.9 7.3 collective-permute-done
  127.2 3.5 collective-permute-done.1
  134.6 7.3 collective-permute-done
  141.9 3.5 collective-permute-done.1
  149.3 7.3 collective-permute-done
  156.6 3.5 collective-permute-done.1
  164.1 7.3 collective-permute-done
  171.3 3.5 collective-permute-done.1
  178.8 7.3 collective-permute-done
  186.1 3.5 collective-permute-done.1
  193.3 259.2 %while.51 = (s32[]{:T(128)}, f32[2,2,3,3,128]{4,0,3,2,1:T(2,128)}, f32[24,8,2,2,3,3,128]{6,1,5,4,3,2,0:T(8,128)S(1)}, f32[24,2,2,3,3,128]{5,1,4,3,2,0:T(2,128)},...) while((s32[]{:T(128)}, f32[2,2,3,3,128]{4,0,3,2,1:T(2,128)}, ...), condition=%wide.region_15.16_spmd, body=%wide.region_2.15_spmd.sunk | while | flops 910086 | bytes 2894023 | solution.py:69
  452.4 2.1 copy.69
  454.6 2.0 reshape.184
  456.6 3.3 fusion.5
  460.9 3.8 multiply_reduce_fusion.27
  466.1 4.2 fusion.7
  470.3 6.0 fusion.6
  476.4 110.9 %while.52 = (s32[]{:T(128)}, f32[8,26,2,3,3,128]{5,0,4,3,2,1:T(8,128)S(1)}, s32[24]{0:T(128)S(1)}, f32[24,2,2,3,3,128]{5,1,4,3,2,0:T(2,128)}, f32[24,8,2,2,3,3,1...) while((s32[]{:T(128)}, f32[8,26,2,3,3,128]{5,0,4,3,2,1:T(8,128)S(1)}, s32[24]{0:T(128)S(1)}, ...), condition=%wide.region_34.35_spmd, body=%wide.region_25.34_spmd.sunk | while | flops 891653 | bytes 3410075 | solution.py:90
  591.9 150.0 %while.53 = (s32[]{:T(128)}, f32[8,2,2,3,3,128]{5,4,3,2,1,0:T(4,128)S(1)}, f32[12,8,2,2,3,3,128]{6,1,5,4,3,2,0:T(8,128)S(1)}, s32[]{:T(128)}) while((s32[]{:T(128)}, f32[8,2,2,3,3,128]{5,4,3,2,1,0:T(4,128)S(1)}, f32[12,8,2,2,3,3,128]{6,1,5,4,3,2,0:T(8,128)S(1)}, s32[]{:T(128)}) %tuple.162), condition=%wide.region_36.37_spmd, body=%wide.region_35.36_spmd.sunk | while | flops 36866 | bytes 1327209 | solution.py:99
  593.9 2.7 collective-permute-done.2
  596.7 10.5 collective-permute-start.2
  607.2 2.7 collective-permute-done.2
  610.0 10.4 collective-permute-start.2
  620.5 2.7 collective-permute-done.2
  623.3 10.5 collective-permute-start.2
  633.8 2.7 collective-permute-done.2
  636.6 10.4 collective-permute-start.2
  647.0 2.7 collective-permute-done.2
  649.8 10.4 collective-permute-start.2
  660.2 2.7 collective-permute-done.2
  663.0 10.4 collective-permute-start.2
  673.4 2.7 collective-permute-done.2
  676.2 10.4 collective-permute-start.2
  686.6 2.6 collective-permute-done.2
  689.3 10.5 collective-permute-start.2
  699.8 2.6 collective-permute-done.2
  702.5 10.5 collective-permute-start.2
  713.0 2.6 collective-permute-done.2
  715.6 10.5 collective-permute-start.2
  726.2 2.6 collective-permute-done.2
  728.8 10.5 collective-permute-start.2
  739.3 2.6 collective-permute-done.2
  742.7 1203.5 %all-gather.3.cloned.1.call-done = f32[32768,192]{1,0:T(8,128)} async-done(((f32[64,192]{1,0:T(8,128)}), f32[32768,192]{1,0:T(8,128)}) %all-gather.3.cloned.1.call-update) | async-done | bytes 25165840 | tf_op jit(solution)/shard_map/all_gather | solution.py:9
  1946.3 12.9 reduce_sum.279
  (1134 shorter events, 330.8 us)
Async XLA Ops:
  7.2 1939.1 %all-gather.3.cloned.1.call-start = ((), (), s32[]{:S(2)}) async-start(), calls=%async_computation | async-start | bytes 33619968 | tf_op jit(solution)/shard_map/all_gather | solution.py:9
  8.9 180.9 %copy-start.2 = (f32[2,2,3,3,128]{4,0,3,2,1:T(2,128)}, f32[2,2,3,3,128]{4,0,3,2,1:T(2,128)S(1)}, u32[]{:S(2)}) copy-start(f32[2,2,3,3,128]{4,0,3,2,1:T(2,128)S(1)} %copy.67) | copy-start | bytes 55300
  12.6 11.1 collective-permute-start
  15.2 12.5 collective-permute-start.1
  27.8 11.1 collective-permute-start
  29.7 12.7 collective-permute-start.1
  42.5 11.1 collective-permute-start
  44.4 12.7 collective-permute-start.1
  57.2 11.1 collective-permute-start
  59.1 12.7 collective-permute-start.1
  71.9 11.1 collective-permute-start
  73.8 12.7 collective-permute-start.1
  86.6 11.1 collective-permute-start
  88.5 12.7 collective-permute-start.1
  101.3 11.1 collective-permute-start
  103.3 12.7 collective-permute-start.1
  116.1 11.1 collective-permute-start
  118.0 12.7 collective-permute-start.1
  130.8 11.1 collective-permute-start
  132.7 12.7 collective-permute-start.1
  145.5 11.1 collective-permute-start
  147.4 12.7 collective-permute-start.1
  160.2 11.1 collective-permute-start
  162.1 12.7 collective-permute-start.1
  174.9 11.1 collective-permute-start
  176.9 12.7 collective-permute-start.1
  189.6 0.9 copy-start.7
  190.6 2.7 copy-start
  459.9 0.9 copy-start.5
  459.9 0.9 copy-start.6
  459.9 1.0 copy-start.8
  459.9 1.0 copy-start.9
  465.0 1.1 copy-start.1
  588.7 1.7 copy-start.3
  588.7 1.8 copy-start.4
  592.0 4.6 collective-permute-start.2
  596.7 13.3 collective-permute-start.2
  610.0 13.2 collective-permute-start.2
  623.3 13.2 collective-permute-start.2
  636.6 13.1 collective-permute-start.2
  649.8 13.1 collective-permute-start.2
  663.0 13.1 collective-permute-start.2
  676.2 13.0 collective-permute-start.2
  689.3 13.1 collective-permute-start.2
  702.5 13.1 collective-permute-start.2
  715.6 13.1 collective-permute-start.2
  728.8 13.1 collective-permute-start.2
Sparse Core Ops, SparseCore 0:
  470.4 1475.8 all-gather.2
